TPU v7x, 256 devices: a whole 4x4x8 slice. The times are simulated.
256 devices in a mesh: span: 8 (over z_lo, y), ulysses: 32 (over x, z_hi, core).
Axes of the slice: x: 4, y: 4, z: 8 (z_hi: 4, z_lo: 2; z = z_hi * 2 + z_lo), core: 2. Of those that a mesh axis runs over, the one named last changes fastest.
Arguments:
- query: bfloat16 [32768, 4096], P(('span', 'ulysses')), may hold values from -32 to 32
- key: bfloat16 [32768, 1024], P(('span', 'ulysses')), may hold values from -6 to 6
- value: bfloat16 [32768, 1024], P(('span', 'ulysses')), may hold values from -6 to 6
- d_out: bfloat16 [32768, 4096], P(('span', 'ulysses')), may hold values from -6 to 6
Outputs:
- attended: bfloat16 [32768, 4096], P(('span', 'ulysses'))
- grad_query: float32 [1024, 4096], P(('span', 'ulysses'))
- grad_key: float32 [1024, 1024], P(('span', 'ulysses'))
- grad_value: float32 [1024, 1024], P(('span', 'ulysses'))
All inputs are finite; a program needn't handle non-finite values.
Results may differ from a plain program's by a relative error of at most 0.0048.
Values may be sent and summed in bfloat16 or wider, within the bound.
A program may use at most 256 MiB of HBM per device.

v0:
```python
import math

import jax
import jax.numpy as jnp
from jax import lax
from jax.sharding import PartitionSpec as P

H = 32
HD = 128
KVH = 8
INTERVAL = 32


def widen(field):
    count = field.shape[0]
    repeat = H // KVH
    spread = jnp.broadcast_to(field.reshape(count, KVH, 1, HD), (count, KVH, repeat, HD))
    return spread.reshape(count, H * HD)


def on_device(query, key, value, d_out):
    tok_rows = query.shape[0]
    n_heads_axis = lax.axis_size("ulysses")
    span_len = tok_rows * n_heads_axis
    per_dev = H // n_heads_axis
    beacons = span_len // INTERVAL
    beacon_dev = tok_rows // INTERVAL
    scale = 1.0 / math.sqrt(HD)
    q_h, k_h, v_h, g_h = (
        lax.all_to_all(query, "ulysses", split_axis=1, concat_axis=0, tiled=True),
        lax.all_to_all(widen(key), "ulysses", split_axis=1, concat_axis=0, tiled=True),
        lax.all_to_all(widen(value), "ulysses", split_axis=1, concat_axis=0, tiled=True),
        lax.all_to_all(d_out, "ulysses", split_axis=1, concat_axis=0, tiled=True),
    )
    own_k = k_h.reshape(beacons, INTERVAL, per_dev * HD)[:, -1]
    own_v = v_h.reshape(beacons, INTERVAL, per_dev * HD)[:, -1]
    prior_k, prior_v = (
        lax.all_gather(own_k, "span", axis=0, tiled=True),
        lax.all_gather(own_v, "span", axis=0, tiled=True),
    )
    all_beacons = prior_k.shape[0]
    mine = lax.axis_index("span")
    visible = jnp.arange(all_beacons) // beacons < mine
    q3 = q_h.reshape(span_len, per_dev, HD)
    k3 = k_h.reshape(span_len, per_dev, HD)
    v3 = v_h.reshape(span_len, per_dev, HD)
    g3 = g_h.reshape(span_len, per_dev, HD)
    pk3 = prior_k.reshape(all_beacons, per_dev, HD)
    pv3 = prior_v.reshape(all_beacons, per_dev, HD)
    own_v3 = v3.reshape(beacons, INTERVAL, per_dev, HD)[:, -1]
    dk_prior = jnp.zeros((all_beacons, per_dev, HD), jnp.float32)
    dv_prior = jnp.zeros((all_beacons, per_dev, HD), jnp.float32)
    dk_own = jnp.zeros((beacons, per_dev, HD), jnp.float32)
    dv_own = jnp.zeros((beacons, per_dev, HD), jnp.float32)
    out_blocks = []
    dq_blocks = []
    block = min(512, span_len)
    n_rows = block // INTERVAL
    for index in range(span_len // block):
        first = index * block
        upper = first + block
        q_blk = q3[first:upper]
        g_blk = g3[first:upper]
        k_loc = k3[:upper]
        v_loc = v3[:upper]
        s_prior = jnp.einsum("qhd,khd->hqk", q_blk, pk3, preferred_element_type=jnp.float32) * scale
        s_prior = jnp.where(visible[None, None, :], s_prior, -jnp.inf)
        s_local = (
            jnp.einsum("qhd,khd->hqk", q_blk, k_loc, preferred_element_type=jnp.float32) * scale
        )
        causal = jnp.arange(upper)[None, :] <= (first + jnp.arange(block))[:, None]
        s_local = jnp.where(causal[None], s_local, -jnp.inf)
        peak = jnp.maximum(jnp.max(s_prior, axis=2), jnp.max(s_local, axis=2))
        e_prior = jnp.exp(s_prior - peak[:, :, None])
        e_local = jnp.exp(s_local - peak[:, :, None])
        denom = jnp.sum(e_prior, axis=2) + jnp.sum(e_local, axis=2)
        p_prior = e_prior / denom[:, :, None]
        p_local = e_local / denom[:, :, None]
        b_prior = p_prior.astype(jnp.bfloat16)
        b_local = p_local.astype(jnp.bfloat16)
        attended = jnp.einsum("hqk,khd->qhd", b_prior, pv3, preferred_element_type=jnp.float32)
        attended = attended + jnp.einsum(
            "hqk,khd->qhd", b_local, v_loc, preferred_element_type=jnp.float32
        )
        out_b = attended.astype(jnp.bfloat16)
        out_blocks.append(out_b)
        delta = jnp.sum(g_blk.astype(jnp.float32) * out_b.astype(jnp.float32), axis=2).T
        dp_prior = jnp.einsum("qhd,khd->hqk", g_blk, pv3, preferred_element_type=jnp.float32)
        ds_prior = (p_prior * (dp_prior - delta[:, :, None])).astype(jnp.bfloat16)
        dk_prior = (
            dk_prior
            + jnp.einsum("hqk,qhd->khd", ds_prior, q_blk, preferred_element_type=jnp.float32)
            * scale
        )
        dv_prior = dv_prior + jnp.einsum(
            "hqk,qhd->khd", b_prior, g_blk, preferred_element_type=jnp.float32
        )
        n_own = upper // INTERVAL
        p_own = p_local.reshape(per_dev, block, n_own, INTERVAL)[..., -1]
        b_own = b_local.reshape(per_dev, block, n_own, INTERVAL)[..., -1]
        dp_own = jnp.einsum(
            "qhd,khd->hqk", g_blk, own_v3[:n_own], preferred_element_type=jnp.float32
        )
        ds_own = (p_own * (dp_own - delta[:, :, None])).astype(jnp.bfloat16)
        dk_own = dk_own.at[:n_own].add(
            jnp.einsum("hqk,qhd->khd", ds_own, q_blk, preferred_element_type=jnp.float32) * scale
        )
        dv_own = dv_own.at[:n_own].add(
            jnp.einsum("hqk,qhd->khd", b_own, g_blk, preferred_element_type=jnp.float32)
        )
        ds_rows_prior = ds_prior.reshape(per_dev, n_rows, INTERVAL, all_beacons)[:, :, -1]
        p_rows_local = p_local.reshape(per_dev, n_rows, INTERVAL, upper)[:, :, -1]
        g_rows = g_blk.reshape(n_rows, INTERVAL, per_dev, HD)[:, -1]
        delta_rows = delta.reshape(per_dev, n_rows, INTERVAL)[:, :, -1]
        dp_rows = jnp.einsum("qhd,khd->hqk", g_rows, v_loc, preferred_element_type=jnp.float32)
        ds_rows_local = (p_rows_local * (dp_rows - delta_rows[:, :, None])).astype(jnp.bfloat16)
        dq_rows = jnp.einsum("hqk,khd->qhd", ds_rows_prior, pk3, preferred_element_type=jnp.float32)
        dq_rows = dq_rows + jnp.einsum(
            "hqk,khd->qhd", ds_rows_local, k_loc, preferred_element_type=jnp.float32
        )
        dq_blocks.append(dq_rows * scale)
    out_heads = jnp.concatenate(out_blocks, 0).reshape(span_len, per_dev * HD)
    attended_tokens = lax.all_to_all(out_heads, "ulysses", split_axis=0, concat_axis=1, tiled=True)
    stacked = jnp.stack(
        [dk_prior.reshape(all_beacons, per_dev * HD), dv_prior.reshape(all_beacons, per_dev * HD)],
        1,
    )
    from_later = lax.psum_scatter(stacked, "span", scatter_dimension=0, tiled=True)
    grad_k_heads = dk_own.reshape(beacons, per_dev * HD) + from_later[:, 0]
    grad_v_heads = dv_own.reshape(beacons, per_dev * HD) + from_later[:, 1]
    grad_q_heads = jnp.concatenate(dq_blocks, 0).reshape(beacons, per_dev * HD)
    grad_q_tok, grad_k_tok, grad_v_tok = (
        lax.all_to_all(grad_q_heads, "ulysses", split_axis=0, concat_axis=1, tiled=True),
        lax.all_to_all(grad_k_heads, "ulysses", split_axis=0, concat_axis=1, tiled=True),
        lax.all_to_all(grad_v_heads, "ulysses", split_axis=0, concat_axis=1, tiled=True),
    )
    repeat = H // KVH
    grad_k_tok = (
        grad_k_tok.reshape(beacon_dev, KVH, repeat, HD).sum(axis=2).reshape(beacon_dev, KVH * HD)
    )
    grad_v_tok = (
        grad_v_tok.reshape(beacon_dev, KVH, repeat, HD).sum(axis=2).reshape(beacon_dev, KVH * HD)
    )
    return (attended_tokens, grad_q_tok, grad_k_tok, grad_v_tok)


def solution(mesh):
    return jax.shard_map(
        on_device,
        mesh=mesh,
        in_specs=(
            P(("span", "ulysses"), None),
            P(("span", "ulysses"), None),
            P(("span", "ulysses"), None),
            P(("span", "ulysses"), None),
        ),
        out_specs=(
            P(("span", "ulysses"), None),
            P(("span", "ulysses"), None),
            P(("span", "ulysses"), None),
            P(("span", "ulysses"), None),
        ),
        check_vma=False,
    )
```

profile of v0, /device:TPU:57, one launch (start us, length us, event | category | flops | bytes accessed | tf_op | source)
XLA Modules:
  0.0 728.5 jit_solution(17974472516163867103)
XLA Ops:
  9.4 10.9 %all-to-all-start.2 = ((bf16[128,32,128]{2,0,1:T(8,128)(2,1)}), bf16[128,32,128]{2,0,1:T(8,128)(2,1)S(1)}, u32[]{:S(2)}, u32[]{:S(2)}) async-start(bf16[128,32,128]{2,0,1:T(8,128)(2,1)} %bitcast.8), calls=%async_computation.2 | async-start | bytes 2097152 | tf_op jit(solution)/shard_map/all_to_all | solution.py:32
  20.3 29.3 %all-to-all-done.2 = bf16[128,32,128]{2,0,1:T(8,128)(2,1)S(1)} async-done(((bf16[128,32,128]{2,0,1:T(8,128)(2,1)}), bf16[128,32,128]{2,0,1:T(8,128)(2,1)S(1)}, u32[]{:S(2)}, u32[]{:S(2)}) %all-to-all-start.2) | async-done | bytes 1048608 | tf_op jit(solution)/shard_map/all_to_all | solution.py:32
  50.8 4.4 all-to-all-start.1
  57.4 27.4 %all-to-all-done.1 = bf16[128,32,128]{2,0,1:T(8,128)(2,1)S(1)} async-done(((bf16[128,32,128]{2,0,1:T(8,128)(2,1)}), bf16[128,32,128]{2,0,1:T(8,128)(2,1)S(1)}, u32[]{:S(2)}, u32[]{:S(2)}) %all-to-all-start.1) | async-done | bytes 1048608 | tf_op jit(solution)/shard_map/all_to_all | solution.py:31
  84.9 4.7 all-to-all-start
  95.6 33.5 %all-gather.1 = bf16[1024,1,128]{2,0,1:T(8,128)(2,1)S(1)} all-gather(bf16[128,1,128]{2,0,1:T(8,128)(2,1)S(1)} %copy.230), channel_id=3, replica_groups=mesh['span'=8,'ulysses'=32] {'span'}, dimensions={0}, use_global_device_ids=true | all-gather | bytes 294912 | tf_op jit(solution)/shard_map/all_gather | solution.py:39
  129.1 16.2 %all-to-all-start.4 = ((bf16[128,32,128]{0,2,1:T(8,128)(2,1)}), bf16[128,32,128]{0,2,1:T(8,128)(2,1)}, u32[]{:S(2)}, u32[]{:S(2)}) async-start(bf16[128,32,128]{0,2,1:T(8,128)(2,1)} %bitcast.868), calls=%async_computation.4 | async-start | bytes 2097152 | tf_op jit(solution)/shard_map/all_to_all | solution.py:33
  149.6 37.2 %all-gather = bf16[1024,1,128]{2,0,1:T(8,128)(2,1)S(1)} all-gather(bf16[128,1,128]{2,0,1:T(8,128)(2,1)S(1)} %copy.228), channel_id=2, replica_groups=mesh['span'=8,'ulysses'=32] {'span'}, dimensions={0}, use_global_device_ids=true | all-gather | bytes 294912 | tf_op jit(solution)/shard_map/all_gather | solution.py:38
  214.0 2.7 fusion.265
  227.6 3.0 slice_convert_fusion
  235.9 6.8 fusion.34
  248.4 3.3 fusion.399
  251.8 3.9 fusion.398
  255.7 4.3 fusion.397
  260.1 5.8 fusion.396
  267.7 5.1 fusion.28
  275.2 3.3 fusion.41
  285.2 4.8 fusion.388
  290.0 3.5 fusion.386
  328.6 4.0 fusion.7
  332.6 4.5 fusion.5
  337.1 4.8 fusion.3
  361.3 7.3 %fusion.384 = (bf16[512,2560]{1,0:T(8,128)(2,1)}, f32[512,2560]{1,0:T(8,128)}) fusion(f32[512]{0:T(512)S(1)} %add.460, f32[512,2560]{1,0:T(8,128)} %get-tuple-element.287, f32[512]{0:T(512)} %copy-done.118), kind=kLoop, calls=%fused_computation.511 | loop fusion | flops 3932160 | bytes 13111296 | tf_op jit(solution)/shard_map/convert_element_type | solution.py:80
  368.7 5.3 fusion.382
  374.3 5.7 fusion.380
  380.2 7.2 fusion.378
  389.1 5.6 fusion.390
  403.7 3.2 multiply_convert_fusion.6
  410.8 2.8 constant_dynamic-update-slice_fusion.5
  414.5 3.3 multiply_convert_fusion.5
  419.1 3.9 copy.293
  423.0 3.2 constant_dynamic-update-slice_fusion.4
  427.0 3.2 multiply_convert_fusion.4
  433.2 4.6 copy.294
  437.8 3.5 constant_dynamic-update-slice_fusion.3
  442.1 3.2 multiply_convert_fusion.3
  448.3 4.6 copy.295
  452.9 3.8 constant_dynamic-update-slice_fusion.2
  457.6 3.2 multiply_convert_fusion.2
  463.7 6.0 copy.296
  469.7 3.9 constant_dynamic-update-slice_fusion.1
  474.4 3.2 multiply_convert_fusion.1
  480.6 6.5 copy.297
  487.1 4.2 constant_dynamic-update-slice_fusion
  492.1 3.2 multiply_convert_fusion
  496.6 3.0 copy.282
  513.0 4.0 copy.283
  520.7 2.6 convolution_add_fusion.11
  525.9 5.4 copy.284
  537.0 2.6 convolution_add_fusion.10
  542.1 5.9 copy.285
  552.2 2.6 convolution_add_fusion.9
  557.3 6.7 copy.286
  570.3 2.6 convolution_add_fusion.8
  575.3 8.5 %copy.287 = f32[512,3584]{0,1:T(8,128)} copy(f32[512,3584]{1,0:T(8,128)} %get-tuple-element.232) | data formatting | bytes 14680064 | tf_op jit(solution)/shard_map/div | solution.py:78
  595.7 9.0 %copy.288 = f32[512,4096]{0,1:T(8,128)} copy(f32[512,4096]{1,0:T(8,128)} %get-tuple-element.230) | data formatting | bytes 16777216 | tf_op jit(solution)/shard_map/div | solution.py:78
  604.7 2.6 slice.845
  623.9 17.0 %all-to-all-start.5 = ((f32[32,4,128]{2,1,0:T(4,128)}), f32[32,4,128]{2,1,0:T(4,128)S(1)}, u32[]{:S(2)}, u32[]{:S(2)}) async-start(f32[32,4,128]{2,1,0:T(4,128)} %bitcast.974), calls=%async_computation.5 | async-start | bytes 131072 | tf_op jit(solution)/shard_map/all_to_all | solution.py:133
  652.6 9.8 %all-to-all-start.3 = ((bf16[32,128,128]{2,1,0:T(8,128)(2,1)}), bf16[32,128,128]{2,1,0:T(8,128)(2,1)S(1)}, u32[]{:S(2)}, u32[]{:S(2)}) async-start(bf16[32,128,128]{2,1,0:T(8,128)(2,1)} %bitcast.964), calls=%async_computation.3 | async-start | bytes 2097152 | tf_op jit(solution)/shard_map/all_to_all | solution.py:123
  672.9 19.2 %all-to-all-done.3 = bf16[32,128,128]{2,1,0:T(8,128)(2,1)S(1)} async-done(((bf16[32,128,128]{2,1,0:T(8,128)(2,1)}), bf16[32,128,128]{2,1,0:T(8,128)(2,1)S(1)}, u32[]{:S(2)}, u32[]{:S(2)}) %all-to-all-start.3) | async-done | bytes 1048608 | tf_op jit(solution)/shard_map/all_to_all | solution.py:123
  692.1 4.4 all-to-all-start.7
  698.5 7.9 %all-to-all-done.7 = f32[32,4,128]{2,1,0:T(4,128)S(1)} async-done(((f32[32,4,128]{2,1,0:T(4,128)}), f32[32,4,128]{2,1,0:T(4,128)S(1)}, u32[]{:S(2)}, u32[]{:S(2)}) %all-to-all-start.7) | async-done | bytes 65568 | tf_op jit(solution)/shard_map/all_to_all | solution.py:135
  706.4 3.9 all-to-all-start.6
  712.1 8.2 %all-to-all-done.6 = f32[32,4,128]{2,1,0:T(4,128)S(1)} async-done(((f32[32,4,128]{2,1,0:T(4,128)}), f32[32,4,128]{2,1,0:T(4,128)S(1)}, u32[]{:S(2)}, u32[]{:S(2)}) %all-to-all-start.6) | async-done | bytes 65568 | tf_op jit(solution)/shard_map/all_to_all | solution.py:134
  (602 shorter events, 262.5 us)
Async XLA Ops:
  7.2 13.1 %copy-start.109 = (bf16[128,1024]{1,0:T(8,128)(2,1)S(1)}, bf16[128,1024]{1,0:T(8,128)(2,1)}, u32[]{:S(2)}) copy-start(bf16[128,1024]{1,0:T(8,128)(2,1)} %param.41) | copy-start | bytes 786436
  9.4 40.2 %all-to-all-start.2 = ((bf16[128,32,128]{2,0,1:T(8,128)(2,1)}), bf16[128,32,128]{2,0,1:T(8,128)(2,1)S(1)}, u32[]{:S(2)}, u32[]{:S(2)}) async-start(bf16[128,32,128]{2,0,1:T(8,128)(2,1)} %bitcast.8), calls=%async_computation.2 | async-start | bytes 2097152 | tf_op jit(solution)/shard_map/all_to_all | solution.py:32
  50.8 34.1 %all-to-all-start.1 = ((bf16[128,32,128]{2,0,1:T(8,128)(2,1)}), bf16[128,32,128]{2,0,1:T(8,128)(2,1)S(1)}, u32[]{:S(2)}, u32[]{:S(2)}) async-start(bf16[128,32,128]{2,0,1:T(8,128)(2,1)} %bitcast.867), calls=%async_computation.1 | async-start | bytes 2097152 | tf_op jit(solution)/shard_map/all_to_all | solution.py:31
  84.9 44.2 %all-to-all-start = ((bf16[128,32,128]{0,2,1:T(8,128)(2,1)}), bf16[128,32,128]{0,2,1:T(8,128)(2,1)}, u32[]{:S(2)}, u32[]{:S(2)}) async-start(bf16[128,32,128]{0,2,1:T(8,128)(2,1)} %bitcast.869), calls=%async_computation | async-start | bytes 2097152 | tf_op jit(solution)/shard_map/all_to_all | solution.py:30
  91.8 144.0 %copy-start.156 = (pred[1024]{0:T(1024)(128)(4,1)}, pred[1024]{0:T(1024)(128)(4,1)S(1)}, u32[]{:S(2)}) copy-start(pred[1024]{0:T(1024)(128)(4,1)S(1)} %fusion.338) | copy-start | bytes 3076
  95.6 52.1 %copy-start.106 = (bf16[4,128,128]{2,1,0:T(8,128)(2,1)}, bf16[4,128,128]{2,1,0:T(8,128)(2,1)S(1)}, u32[]{:S(2)}) copy-start(bf16[4,128,128]{2,1,0:T(8,128)(2,1)S(1)} %slice.786) | copy-start | bytes 393220
  129.1 98.5 %all-to-all-start.4 = ((bf16[128,32,128]{0,2,1:T(8,128)(2,1)}), bf16[128,32,128]{0,2,1:T(8,128)(2,1)}, u32[]{:S(2)}, u32[]{:S(2)}) async-start(bf16[128,32,128]{0,2,1:T(8,128)(2,1)} %bitcast.868), calls=%async_computation.4 | async-start | bytes 2097152 | tf_op jit(solution)/shard_map/all_to_all | solution.py:33
  145.3 526.0 %reduce-scatter.2.cloned.1.call-start = ((), (), s32[]{:S(2)}) async-start(), calls=%async_computation.9 | async-start | bytes 1179648 | tf_op jit(solution)/shard_map/reduce_scatter | solution.py:128
  235.8 30.2 %copy-start.32 = (f32[512,1024]{1,0:T(8,128)}, f32[512,1024]{1,0:T(8,128)S(1)}, u32[]{:S(2)}) copy-start(f32[512,1024]{1,0:T(8,128)S(1)} %get-tuple-element.279) | copy-start | bytes 6291460
  242.6 23.3 %copy-start.27 = (f32[512,1024]{1,0:T(8,128)}, f32[512,1024]{1,0:T(8,128)S(1)}, u32[]{:S(2)}) copy-start(f32[512,1024]{1,0:T(8,128)S(1)} %get-tuple-element.277) | copy-start | bytes 6291460
  242.7 23.3 %copy-start.149 = (f32[512]{0:T(512)}, f32[512]{0:T(512)S(1)}, u32[]{:S(2)}) copy-start(f32[512]{0:T(512)S(1)} %max.73) | copy-start | bytes 6148
  243.7 30.2 %copy-start.127 = (f32[512]{0:T(512)}, f32[512]{0:T(512)S(1)}, u32[]{:S(2)}) copy-start(f32[512]{0:T(512)S(1)} %max.74) | copy-start | bytes 6148
  251.7 76.9 %copy-start.118 = (f32[512]{0:T(512)}, f32[512]{0:T(512)S(1)}, u32[]{:S(2)}) copy-start(f32[512]{0:T(512)S(1)} %max.76) | copy-start | bytes 6148
  255.7 77.0 %copy-start.120 = (f32[512]{0:T(512)}, f32[512]{0:T(512)S(1)}, u32[]{:S(2)}) copy-start(f32[512]{0:T(512)S(1)} %max.77) | copy-start | bytes 6148
  260.0 77.1 %copy-start.122 = (f32[512]{0:T(512)}, f32[512]{0:T(512)S(1)}, u32[]{:S(2)}) copy-start(f32[512]{0:T(512)S(1)} %max.78) | copy-start | bytes 6148
  328.6 13.3 %slice-start = ((s8[8388608]{0:T(1024)(128)(4,1)}), s8[4194304]{0:T(1024)(128)(4,1)S(1)}, s32[]{:S(2)}) async-start(s8[8388608]{0:T(1024)(128)(4,1)} %bitcast.820), calls=%async_computation.10 | async-start | bytes 8388608
  332.6 9.3 %slice-start.1 = ((s8[8388608]{0:T(1024)(128)(4,1)}), s8[4194304]{0:T(1024)(128)(4,1)S(1)}, s32[]{:S(2)}) async-start(s8[8388608]{0:T(1024)(128)(4,1)} %bitcast.820), calls=%async_computation.11 | async-start | bytes 8388608
  359.8 8.8 %copy-start.117 = (f32[16,1,128]{2,0,1:T(8,128)}, f32[16,1,128]{2,0,1:T(8,128)S(1)}, u32[]{:S(2)}) copy-start(f32[16,1,128]{2,0,1:T(8,128)S(1)} %fusion.162) | copy-start | bytes 24580
  360.4 8.2 %slice-start.6 = ((s8[6291456]{0:T(1024)(128)(4,1)}), s8[4194304]{0:T(1024)(128)(4,1)S(1)}, s32[]{:S(2)}) async-start(s8[6291456]{0:T(1024)(128)(4,1)} %bitcast.838), calls=%async_computation.16 | async-start | bytes 8388608
  380.2 8.3 %copy-start.28 = (f32[512,1024]{1,0:T(8,128)S(1)}, f32[512,1024]{1,0:T(8,128)}, u32[]{:S(2)}) copy-start(f32[512,1024]{1,0:T(8,128)} %copy-done.27) | copy-start | bytes 6291460
  380.2 8.9 %copy-start.33 = (f32[512,1024]{1,0:T(8,128)S(1)}, f32[512,1024]{1,0:T(8,128)}, u32[]{:S(2)}) copy-start(f32[512,1024]{1,0:T(8,128)} %copy-done.32) | copy-start | bytes 6291460
  380.2 8.9 %copy-start.119 = (f32[512]{0:T(512)S(1)}, f32[512]{0:T(512)}, u32[]{:S(2)}) copy-start(f32[512]{0:T(512)} %copy-done.118) | copy-start | bytes 6148
  380.2 8.9 %copy-start.150 = (f32[512]{0:T(512)S(1)}, f32[512]{0:T(512)}, u32[]{:S(2)}) copy-start(f32[512]{0:T(512)} %copy-done.149) | copy-start | bytes 6148
  380.2 8.9 %copy-start.158 = (pred[1024]{0:T(1024)(128)(4,1)S(1)}, pred[1024]{0:T(1024)(128)(4,1)}, u32[]{:S(2)}) copy-start(pred[1024]{0:T(1024)(128)(4,1)} %copy-done.156) | copy-start | bytes 3076
  499.6 10.6 %copy-start.35 = (bf16[512,1024]{1,0:T(8,128)(2,1)S(1)}, bf16[512,1024]{1,0:T(8,128)(2,1)}, u32[]{:S(2)}) copy-start(bf16[512,1024]{1,0:T(8,128)(2,1)} %multiply_convert_fusion.5) | copy-start | bytes 3145732
  499.6 10.6 %copy-start.71 = (bf16[4,128,128]{2,1,0:T(8,128)(2,1)S(1)}, bf16[4,128,128]{2,1,0:T(8,128)(2,1)}, u32[]{:S(2)}) copy-start(bf16[4,128,128]{2,1,0:T(8,128)(2,1)} %copy.232) | copy-start | bytes 393220
  517.0 8.1 %copy-start.144 = (f32[1,16,32]{2,1,0:T(8,128)S(1)}, f32[1,16,32]{2,1,0:T(8,128)}, u32[]{:S(2)}) copy-start(f32[1,16,32]{2,1,0:T(8,128)} %reshape_transpose.27) | copy-start | bytes 6148
  525.9 11.2 %copy-start.79 = (bf16[4,128,128]{2,1,0:T(8,128)(2,1)S(1)}, bf16[4,128,128]{2,1,0:T(8,128)(2,1)}, u32[]{:S(2)}) copy-start(bf16[4,128,128]{2,1,0:T(8,128)(2,1)} %copy.234) | copy-start | bytes 393220
  531.3 10.1 %copy-start.145 = (f32[1,16,32]{2,1,0:T(8,128)S(1)}, f32[1,16,32]{2,1,0:T(8,128)}, u32[]{:S(2)}) copy-start(f32[1,16,32]{2,1,0:T(8,128)} %reshape_transpose.28) | copy-start | bytes 6148
  542.1 10.1 %copy-start.75 = (bf16[4,128,128]{2,1,0:T(8,128)(2,1)S(1)}, bf16[4,128,128]{2,1,0:T(8,128)(2,1)}, u32[]{:S(2)}) copy-start(bf16[4,128,128]{2,1,0:T(8,128)(2,1)} %copy.235) | copy-start | bytes 393220
  548.0 8.5 %copy-start.146 = (f32[1,16,32]{2,1,0:T(8,128)S(1)}, f32[1,16,32]{2,1,0:T(8,128)}, u32[]{:S(2)}) copy-start(f32[1,16,32]{2,1,0:T(8,128)} %reshape_transpose.29) | copy-start | bytes 6148
  557.3 12.9 %copy-start.67 = (bf16[4,128,128]{2,1,0:T(8,128)(2,1)S(1)}, bf16[4,128,128]{2,1,0:T(8,128)(2,1)}, u32[]{:S(2)}) copy-start(bf16[4,128,128]{2,1,0:T(8,128)(2,1)} %copy.236) | copy-start | bytes 393220
  564.0 10.6 %copy-start.147 = (f32[1,16,32]{2,1,0:T(8,128)S(1)}, f32[1,16,32]{2,1,0:T(8,128)}, u32[]{:S(2)}) copy-start(f32[1,16,32]{2,1,0:T(8,128)} %reshape_transpose.30) | copy-start | bytes 6148
  575.3 14.8 %copy-start.57 = (bf16[4,128,128]{2,1,0:T(8,128)(2,1)S(1)}, bf16[4,128,128]{2,1,0:T(8,128)(2,1)}, u32[]{:S(2)}) copy-start(bf16[4,128,128]{2,1,0:T(8,128)(2,1)} %copy.237) | copy-start | bytes 393220
  604.7 8.7 %copy-start.34 = (bf16[16,128,128]{2,1,0:T(8,128)(2,1)S(1)}, bf16[16,128,128]{2,1,0:T(8,128)(2,1)}, u32[]{:S(2)}) copy-start(bf16[16,128,128]{2,1,0:T(8,128)(2,1)} %slice.797) | copy-start | bytes 1572868
  622.7 28.5 %copy-start.51 = (bf16[4,128,128]{2,1,0:T(8,128)(2,1)S(1)}, bf16[4,128,128]{2,1,0:T(8,128)(2,1)}, u32[]{:S(2)}) copy-start(bf16[4,128,128]{2,1,0:T(8,128)(2,1)} %copy.245) | copy-start | bytes 393220
  622.7 28.5 %copy-start.93 = (f32[128,1,128]{2,0,1:T(8,128)S(1)}, f32[128,1,128]{2,0,1:T(8,128)}, u32[]{:S(2)}) copy-start(f32[128,1,128]{2,0,1:T(8,128)} %scatter-add.59) | copy-start | bytes 196612
  622.7 28.5 %copy-start.114 = (bf16[1,512,32,1]{1,3,2,0:T(2,128)(2,1)S(1)}, bf16[1,512,32,1]{1,3,2,0:T(2,128)(2,1)}, u32[]{:S(2)}) copy-start(bf16[1,512,32,1]{1,3,2,0:T(2,128)(2,1)} %slice.871) | copy-start | bytes 98308
  622.8 28.6 %copy-start.39 = (bf16[4,128,128]{2,1,0:T(8,128)(2,1)S(1)}, bf16[4,128,128]{2,1,0:T(8,128)(2,1)}, u32[]{:S(2)}) copy-start(bf16[4,128,128]{2,1,0:T(8,128)(2,1)} %copy.250) | copy-start | bytes 393220
  622.8 28.6 %copy-start.112 = (bf16[1,512,48,1]{1,3,2,0:T(2,128)(2,1)S(1)}, bf16[1,512,48,1]{1,3,2,0:T(2,128)(2,1)}, u32[]{:S(2)}) copy-start(bf16[1,512,48,1]{1,3,2,0:T(2,128)(2,1)} %slice.873) | copy-start | bytes 147460
  623.9 27.6 %copy-start.49 = (bf16[4,128,128]{2,1,0:T(8,128)(2,1)S(1)}, bf16[4,128,128]{2,1,0:T(8,128)(2,1)}, u32[]{:S(2)}) copy-start(bf16[4,128,128]{2,1,0:T(8,128)(2,1)} %copy.255) | copy-start | bytes 393220
  623.9 27.6 %copy-start.108 = (bf16[1,512,64,1]{1,3,2,0:T(2,128)(2,1)S(1)}, bf16[1,512,64,1]{1,3,2,0:T(2,128)(2,1)}, u32[]{:S(2)}) copy-start(bf16[1,512,64,1]{1,3,2,0:T(2,128)(2,1)} %slice.875) | copy-start | bytes 196612
  623.9 27.8 %copy-start.47 = (bf16[4,128,128]{2,1,0:T(8,128)(2,1)S(1)}, bf16[4,128,128]{2,1,0:T(8,128)(2,1)}, u32[]{:S(2)}) copy-start(bf16[4,128,128]{2,1,0:T(8,128)(2,1)} %copy.260) | copy-start | bytes 393220
  623.9 27.8 %copy-start.107 = (bf16[1,512,80,1]{1,3,2,0:T(2,128)(2,1)S(1)}, bf16[1,512,80,1]{1,3,2,0:T(2,128)(2,1)}, u32[]{:S(2)}) copy-start(bf16[1,512,80,1]{1,3,2,0:T(2,128)(2,1)} %slice.877) | copy-start | bytes 245764
  623.9 28.0 %all-to-all-start.5 = ((f32[32,4,128]{2,1,0:T(4,128)}), f32[32,4,128]{2,1,0:T(4,128)S(1)}, u32[]{:S(2)}, u32[]{:S(2)}) async-start(f32[32,4,128]{2,1,0:T(4,128)} %bitcast.974), calls=%async_computation.5 | async-start | bytes 131072 | tf_op jit(solution)/shard_map/all_to_all | solution.py:133
  649.1 13.3 %copy-start.45 = (bf16[4,128,128]{2,1,0:T(8,128)(2,1)S(1)}, bf16[4,128,128]{2,1,0:T(8,128)(2,1)}, u32[]{:S(2)}) copy-start(bf16[4,128,128]{2,1,0:T(8,128)(2,1)} %copy.265) | copy-start | bytes 393220
  649.1 14.4 %copy-start.87 = (bf16[4,128,128]{2,1,0:T(8,128)(2,1)S(1)}, bf16[4,128,128]{2,1,0:T(8,128)(2,1)}, u32[]{:S(2)}) copy-start(bf16[4,128,128]{2,1,0:T(8,128)(2,1)} %copy.231) | copy-start | bytes 393220
  649.1 14.4 %copy-start.92 = (f32[128,1,128]{2,0,1:T(8,128)S(1)}, f32[128,1,128]{2,0,1:T(8,128)}, u32[]{:S(2)}) copy-start(f32[128,1,128]{2,0,1:T(8,128)} %scatter-add.46) | copy-start | bytes 196612
  651.0 13.6 %copy-start.43 = (bf16[4,128,128]{2,1,0:T(8,128)(2,1)S(1)}, bf16[4,128,128]{2,1,0:T(8,128)(2,1)}, u32[]{:S(2)}) copy-start(bf16[4,128,128]{2,1,0:T(8,128)(2,1)} %copy.270) | copy-start | bytes 393220
  651.2 14.7 %copy-start.72 = (bf16[4,128,128]{2,1,0:T(8,128)(2,1)S(1)}, bf16[4,128,128]{2,1,0:T(8,128)(2,1)}, u32[]{:S(2)}) copy-start(bf16[4,128,128]{2,1,0:T(8,128)(2,1)} %copy.232) | copy-start | bytes 393220
  651.6 15.5 %copy-start.84 = (bf16[4,128,128]{2,1,0:T(8,128)(2,1)S(1)}, bf16[4,128,128]{2,1,0:T(8,128)(2,1)}, u32[]{:S(2)}) copy-start(bf16[4,128,128]{2,1,0:T(8,128)(2,1)} %copy.233) | copy-start | bytes 393220
  651.9 16.4 %copy-start.80 = (bf16[4,128,128]{2,1,0:T(8,128)(2,1)S(1)}, bf16[4,128,128]{2,1,0:T(8,128)(2,1)}, u32[]{:S(2)}) copy-start(bf16[4,128,128]{2,1,0:T(8,128)(2,1)} %copy.234) | copy-start | bytes 393220
  651.9 17.6 %copy-start.76 = (bf16[4,128,128]{2,1,0:T(8,128)(2,1)S(1)}, bf16[4,128,128]{2,1,0:T(8,128)(2,1)}, u32[]{:S(2)}) copy-start(bf16[4,128,128]{2,1,0:T(8,128)(2,1)} %copy.235) | copy-start | bytes 393220
  651.9 17.6 %copy-start.116 = (bf16[96,1,1,128]{3,1,0,2:T(2,128)(2,1)S(1)}, bf16[96,1,1,128]{3,1,0,2:T(2,128)(2,1)}, u32[]{:S(2)}) copy-start(bf16[96,1,1,128]{3,1,0,2:T(2,128)(2,1)} %slice.863) | copy-start | bytes 73732
  652.0 18.9 %copy-start.68 = (bf16[4,128,128]{2,1,0:T(8,128)(2,1)S(1)}, bf16[4,128,128]{2,1,0:T(8,128)(2,1)}, u32[]{:S(2)}) copy-start(bf16[4,128,128]{2,1,0:T(8,128)(2,1)} %copy.236) | copy-start | bytes 393220
  652.6 39.6 %all-to-all-start.3 = ((bf16[32,128,128]{2,1,0:T(8,128)(2,1)}), bf16[32,128,128]{2,1,0:T(8,128)(2,1)S(1)}, u32[]{:S(2)}, u32[]{:S(2)}) async-start(bf16[32,128,128]{2,1,0:T(8,128)(2,1)} %bitcast.964), calls=%async_computation.3 | async-start | bytes 2097152 | tf_op jit(solution)/shard_map/all_to_all | solution.py:123
  662.4 8.8 %copy-start.41 = (bf16[4,128,128]{2,1,0:T(8,128)(2,1)S(1)}, bf16[4,128,128]{2,1,0:T(8,128)(2,1)}, u32[]{:S(2)}) copy-start(bf16[4,128,128]{2,1,0:T(8,128)(2,1)} %copy.275) | copy-start | bytes 393220
  662.4 34.2 %copy-start.58 = (bf16[4,128,128]{2,1,0:T(8,128)(2,1)S(1)}, bf16[4,128,128]{2,1,0:T(8,128)(2,1)}, u32[]{:S(2)}) copy-start(bf16[4,128,128]{2,1,0:T(8,128)(2,1)} %copy.237) | copy-start | bytes 393220
  664.7 31.9 %copy-start.113 = (bf16[128,1,1,128]{3,1,0,2:T(2,128)(2,1)S(1)}, bf16[128,1,1,128]{3,1,0,2:T(2,128)(2,1)}, u32[]{:S(2)}) copy-start(bf16[128,1,1,128]{3,1,0,2:T(2,128)(2,1)} %slice.868) | copy-start | bytes 98308
  664.7 31.9 %copy-start.134 = (f32[512]{0:T(512)S(1)}, f32[512]{0:T(512)}, u32[]{:S(2)}) copy-start(f32[512]{0:T(512)} %copy-done.133) | copy-start | bytes 6148
  670.8 50.0 %copy-start.111 = (f32[32,4,128]{2,1,0:T(4,128)S(1)}, f32[32,4,128]{2,1,0:T(4,128)}, u32[]{:S(2)}) copy-start(f32[32,4,128]{2,1,0:T(4,128)} %copy-done.110) | copy-start | bytes 196612
  670.9 50.6 %copy-start.1 = (bf16[128,1024]{1,0:T(8,128)(2,1)S(1)}, bf16[128,1024]{1,0:T(8,128)(2,1)}, u32[]{:S(2)}) copy-start(bf16[128,1024]{1,0:T(8,128)(2,1)} %param.42) | copy-start | bytes 786436
  692.1 14.3 %all-to-all-start.7 = ((f32[32,4,128]{2,1,0:T(4,128)}), f32[32,4,128]{2,1,0:T(4,128)S(1)}, u32[]{:S(2)}, u32[]{:S(2)}) async-start(f32[32,4,128]{2,1,0:T(4,128)} %bitcast.242), calls=%async_computation.8 | async-start | bytes 131072 | tf_op jit(solution)/shard_map/all_to_all | solution.py:135
  706.4 13.8 %all-to-all-start.6 = ((f32[32,4,128]{2,1,0:T(4,128)}), f32[32,4,128]{2,1,0:T(4,128)S(1)}, u32[]{:S(2)}, u32[]{:S(2)}) async-start(f32[32,4,128]{2,1,0:T(4,128)} %bitcast.204), calls=%async_computation.7 | async-start | bytes 131072 | tf_op jit(solution)/shard_map/all_to_all | solution.py:134
  (128 other events, 550.4 us)
Sparse Core Ops, SparseCore 0:
  595.0 43.0 reduce-scatter.1
where the time goes:
time: 741 us; the launch traced here: 729 us
  local copies, waits for them, and re-layouts  236 us (32%)
  matrix products  165 us (22%)
  waiting for transfers between devices  92.1 us (12%)
  other arithmetic  77.3 us (10%)
  starting transfers between devices  71.2 us (10%)
  blocking collectives  70.7 us (10%)
  between operations  16.1 us (2%)
    div x8, local copies, waits for them, and re-layouts, on_device(): p_local = e_local / denom[:, :, None]  45.1 us
    convert_element_type x8, other arithmetic, on_device(): b_local = p_local.astype(jnp.bfloat16)  40.5 us
    all_gather x1, blocking collectives, on_device(): lax.all_gather(own_k, 'span', axis=0, tiled=True)  37.2 us
    all_gather x1, blocking collectives, on_device(): lax.all_gather(own_v, 'span', axis=0, tiled=True)  33.5 us
    convert_element_type x7, local copies, waits for them, and re-layouts, on_device(): b_local = p_local.astype(jnp.bfloat16)  30.5 us
    all_to_all x1, waiting for transfers between devices, on_device(): lax.all_to_all(widen(value), 'ulysses', split_axis=1, concat_axis=0, tile...  29.3 us
    all_to_all x1, waiting for transfers between devices, on_device(): lax.all_to_all(widen(key), 'ulysses', split_axis=1, concat_axis=0, tiled=...  27.4 us
    dot_general x8, matrix products, on_device(): jnp.einsum('hqk,khd->qhd', b_local, v_loc, preferred_element_type=jnp.flo...  24.8 us
  transfers between devices with their start and end apart: 9, of which 5 were waited for; matrix products, arithmetic and copies ran while one was open for 15% of the time, Pallas kernels for 0%

commit v1 on v0

v1 whole, which is shorter than its diff:
```python
import functools
import math

import jax
import jax.numpy as jnp
from jax import lax
from jax.experimental import pallas as pl
from jax.experimental.pallas import tpu as pltpu
from jax.sharding import PartitionSpec as P

NX, NZ, NC, NS = 4, 4, 2, 8
NG = NX * NC
HD = 128
REP = 4
TOK = 128
BLK = NC * TOK
STEP = NZ * BLK
LOC = NX * STEP
ROWS = REP * BLK
BEA = 32
BSP = BEA * NZ
ALLB = NS * BSP
PLANE = NS * NZ
SCALE = 1.0 / math.sqrt(HD)
LOG2E = 1.4426950408889634
C2 = SCALE * LOG2E
MESH = pl.DeviceIdType.MESH
COMM = True
FWD = True
BWD = True


def dot_t(a, b):
    return lax.dot_general(a, b, (((1,), (1,)), ((), ())), preferred_element_type=jnp.float32)


def dot_n(a, b):
    return lax.dot_general(a, b, (((1,), (0,)), ((), ())), preferred_element_type=jnp.float32)


def iota(shape, dim):
    return lax.broadcasted_iota(jnp.int32, shape, dim)


def fused(
    q_hbm, k_hbm, v_hbm, do_hbm,
    out_hbm, gq_ref, gk_ref, gv_ref,
    kv, kvb, bst, qg, dog, outg, q4, do4, sbuf, mx, acc, lse_row, del_row,
    dk_acc, dv_acc, gacc, slots, tiles, gkv_in, dq_st, gq_in,
    kx_s, kx_r, vx_s, vx_r, q_s, q_r, do_s, do_r, z_s, z_r, zr_s, b_s, b_r,
    o_s, o_r, g_s, g_r, t_s, t_r, d_s, d_r,
):
    c = lax.axis_index("span")
    u = lax.axis_index("ulysses")
    x = u // (NZ * NC)
    z = (u // NC) % NZ
    core = u % NC
    g = x * NC + core
    me = c * NZ + z
    zp, zm = (z + 1) % NZ, (z + NZ - 1) % NZ

    def uly(grp, zz):
        return (grp // NC) * (NZ * NC) + zz * NC + grp % NC

    def in_group(grp):
        return {"span": c, "ulysses": uly(grp, z)}

    def in_plane(s):
        return {"span": s // NZ, "ulysses": uly(g, s % NZ)}

    def remote(src, dst, ssem, rsem, dev):
        return pltpu.make_async_remote_copy(
            src_ref=src, dst_ref=dst, send_sem=ssem, recv_sem=rsem, device_id=dev, device_id_type=MESH
        )

    def arrived(dst, sem):
        pltpu.make_async_copy(dst, dst, sem).wait()

    def kv_rows(grp, zz):
        return pl.ds((grp // NC) * STEP + zz * BLK + (grp % NC) * TOK, TOK)

    def piece_k(grp):
        return kv.at[kv_rows(grp, z), pl.ds(0, HD)]

    def piece_v(grp):
        return kv.at[kv_rows(grp, z), pl.ds(HD, HD)]

    def piece_q(buf, grp):
        return buf.at[pl.ds(grp * TOK, TOK), :]

    def x_copies(to, src_k=True):
        cols = pl.ds(pl.multiple_of(to * HD, HD), HD)
        wide = pl.ds(pl.multiple_of(to * REP * HD, REP * HD), REP * HD)
        return (
            (k_hbm.at[:, cols], piece_k(g), kx_s.at[to], kx_r.at[g]),
            (v_hbm.at[:, cols], piece_v(g), vx_s.at[to], vx_r.at[g]),
            (q_hbm.at[:, wide], piece_q(qg, g), q_s.at[to], q_r.at[g]),
            (do_hbm.at[:, wide], piece_q(dog, g), do_s.at[to], do_r.at[g]),
        )

    def z_rows(xx, zz):
        return pl.ds(xx * STEP + zz * BLK, BLK)

    def z_piece(xx, zz, lo, width):
        return kv.at[z_rows(xx, zz), pl.ds(lo, width)]

    def z_dev(zz):
        return {"span": c, "ulysses": uly(g, zz)}

    def z_send(xx, way):
        to = zp if way == 0 else zm
        part = z_piece(xx, z, 0, 2 * HD)
        return remote(part, part, z_s.at[xx, way], z_r.at[xx, way], z_dev(to))

    def z_relay(xx, way):
        to, of = (zp, zm) if way == 0 else (zm, zp)
        part = z_piece(xx, of, way * HD, HD)
        return remote(part, part, zr_s.at[xx, way], z_r.at[xx, 2 + way], z_dev(to))

    def b_rows(s):
        return kvb.at[pl.ds(pl.multiple_of(s * BEA, BEA), BEA), pl.ds(0, 2 * HD)]

    def b_send(s):
        return remote(bst, b_rows(me), b_s.at[s], b_r.at[me], in_plane(s))

    def o_send(grp):
        dst = out_hbm.at[:, pl.ds(pl.multiple_of(g * REP * HD, REP * HD), REP * HD)]
        return remote(piece_q(outg, grp), dst, o_s.at[grp], o_r.at[g], in_group(grp))

    def g_send(s):
        return remote(gacc.at[s], slots.at[me], g_s.at[s], g_r.at[me], in_plane(s))

    def t_send(grp):
        return remote(tiles.at[grp], gkv_in.at[g], t_s.at[grp], t_r.at[g], in_group(grp))

    def d_send(grp):
        return remote(
            dq_st.at[pl.ds(pl.multiple_of(grp * 16, 16), 16), :],
            gq_in.at[pl.ds(pl.multiple_of(g * 16, 16), 16), :],
            d_s.at[grp], d_r.at[g], in_group(grp),
        )

    def others(body):
        for k in range(1, NG):
            body((g + k) % NG)

    def plane(lo, hi, body):
        def one(s, carry):
            @pl.when(s != me)
            def _():
                body(s)

            return carry

        lax.fori_loop(lo, hi, one, 0)

    if COMM:
        barrier = pltpu.get_barrier_semaphore()
        others(lambda grp: pl.semaphore_signal(barrier, inc=1, device_id=in_group(grp), device_id_type=MESH))
        plane(0, PLANE, lambda s: pl.semaphore_signal(barrier, inc=1, device_id=in_plane(s), device_id_type=MESH))
        pl.semaphore_wait(barrier, NG - 1 + PLANE - 1)

    mine = x_copies(g)
    for which in range(4):
        src, dst, _, rsem = mine[which]
        pltpu.make_async_copy(src, dst, rsem).start()
        if COMM:
            others(lambda grp, which=which: remote(*x_copies(grp)[which], in_group(grp)).start())

    kv[:, pl.ds(2 * HD, HD)] = jnp.ones((LOC, HD), jnp.bfloat16)
    kvb[:, pl.ds(2 * HD, HD)] = jnp.ones((ALLB, HD), jnp.bfloat16)

    def wait_group(buf_piece, sem, grp):
        arrived(buf_piece(grp), sem.at[grp])

    for xx in range(NX):
        for cc in range(NC):
            grp = xx * NC + cc
            if COMM:
                wait_group(piece_k, kx_r, grp)
                wait_group(piece_v, vx_r, grp)
        if COMM:
            z_send(xx, 0).start()
            z_send(xx, 1).start()
    if not COMM:
        wait_group(piece_k, kx_r, g)
        wait_group(piece_v, vx_r, g)

    picked = jnp.zeros((BEA, 2 * HD), jnp.float32)
    for xx in range(NX):
        row, col = iota((BEA, BLK), 0), iota((BEA, BLK), 1)
        hot = (row * 32 + 31 == col + xx * BLK).astype(jnp.bfloat16)
        picked = picked + dot_n(hot, kv[z_rows(xx, z), pl.ds(0, 2 * HD)])
    bst[...] = picked.astype(jnp.bfloat16)
    kvb[pl.ds(pl.multiple_of(me * BEA, BEA), BEA), pl.ds(0, 2 * HD)] = bst[...]
    if COMM:
        plane(c * NZ, PLANE, lambda s: b_send(s).start())
        for xx in range(NX):
            arrived(z_piece(xx, zm, 0, 2 * HD), z_r.at[xx, 0])
            z_relay(xx, 0).start()
            arrived(z_piece(xx, zp, 0, 2 * HD), z_r.at[xx, 1])
            z_relay(xx, 1).start()
        plane(0, (c + 1) * NZ, lambda s: arrived(b_rows(s), b_r.at[s]))

    n_prior = (c + 1) // 2
    z2 = (z + 2) % NZ

    def block(i, carry):
        for cc in range(NC):
            grp = i * NC + cc
            if COMM:
                wait_group(functools.partial(piece_q, qg), q_r, grp)
            else:
                pl.when(grp == g)(lambda: wait_group(functools.partial(piece_q, qg), q_r, g))
        if COMM:
            arrived(z_piece(i, z2, 0, HD), z_r.at[i, 2])
            arrived(z_piece(i, z2, HD, HD), z_r.at[i, 3])
        for h in range(REP):
            q4[i, pl.ds(h * BLK, BLK), :] = qg[pl.ds(i * BLK, BLK), pl.ds(h * HD, HD)]
        if not FWD:
            return carry
        mx[...] = jnp.full((ROWS, HD), -jnp.inf, jnp.float32)

        def widest(s, rows):
            top = s[:, :HD]
            for t in range(1, s.shape[1] // HD):
                top = jnp.maximum(top, s[:, t * HD : (t + 1) * HD])
            mx[rows, :] = jnp.maximum(mx[rows, :], top)

        def score_prior(jp, cr):
            keys = kvb[pl.ds(pl.multiple_of(jp * 256, 256), 256), pl.ds(0, HD)]
            for h in range(REP):
                rows = pl.ds(h * BLK, BLK)
                s = dot_t(q4[i, rows, :], keys)
                s = jnp.where(iota(s.shape, 1) < c * BSP - jp * 256, s, -jnp.inf)
                sbuf[0, rows, pl.ds(pl.multiple_of(jp * 256, 256), 256)] = s
                widest(s, rows)
            return cr

        lax.fori_loop(0, n_prior, score_prior, 0)

        def score(j, masked):
            keys = kv[pl.ds(pl.multiple_of(j * STEP, STEP), STEP), pl.ds(0, HD)]
            for h in range(REP):
                rows = pl.ds(h * BLK, BLK)
                s = dot_t(q4[i, rows, :], keys)
                if masked:
                    s = jnp.where(iota(s.shape, 1) - iota(s.shape, 0) <= z * BLK, s, -jnp.inf)
                sbuf[1 + j, rows, :] = s
                widest(s, rows)

        def score_full(j, cr):
            score(j, False)
            return cr

        lax.fori_loop(0, i, score_full, 0)
        score(i, True)

        peak = jnp.max(mx[...], axis=1, keepdims=True) * C2
        mx[...] = jnp.broadcast_to(peak, (ROWS, HD))
        acc[...] = jnp.zeros((ROWS, 2 * HD), jnp.float32)

        def spread(s, rows):
            m = mx[rows, :]
            return jnp.concatenate(
                [jnp.exp2(s[:, t * HD : (t + 1) * HD] * C2 - m) for t in range(s.shape[1] // HD)], axis=1
            ).astype(jnp.bfloat16)

        def mix_prior(jp, cr):
            at = pl.ds(pl.multiple_of(jp * 256, 256), 256)
            vals = kvb[at, pl.ds(HD, 2 * HD)]
            for h in range(REP):
                rows = pl.ds(h * BLK, BLK)
                acc[rows, :] += dot_n(spread(sbuf[0, rows, at], rows), vals)
            return cr

        lax.fori_loop(0, n_prior, mix_prior, 0)

        def mix(j, cr):
            vals = kv[pl.ds(pl.multiple_of(j * STEP, STEP), STEP), pl.ds(HD, 2 * HD)]
            for h in range(REP):
                rows = pl.ds(h * BLK, BLK)
                acc[rows, :] += dot_n(spread(sbuf[1 + j, rows, :], rows), vals)
            return cr

        lax.fori_loop(0, i + 1, mix, 0)
        eye = iota((HD, HD), 0) == iota((HD, HD), 1)
        for h in range(REP):
            rows = pl.ds(h * BLK, BLK)
            total = acc[rows, pl.ds(HD, HD)]
            outg[pl.ds(i * BLK, BLK), pl.ds(h * HD, HD)] = (acc[rows, pl.ds(0, HD)] / total).astype(jnp.bfloat16)
            lse = mx[rows, :] + jnp.log2(total)
            for t in range(BLK // HD):
                part = jnp.where(eye, lse[t * HD : (t + 1) * HD], 0.0)
                lse_row[i, :, pl.ds(h * BLK + t * HD, HD)] = jnp.sum(part, axis=0, keepdims=True)
        for cc in range(NC):
            grp = i * NC + cc

            @pl.when(grp != g)
            def _():
                if COMM:
                    o_send(grp).start()

            @pl.when(grp == g)
            def _():
                cols = pl.ds(pl.multiple_of(g * REP * HD, REP * HD), REP * HD)
                pltpu.make_async_copy(piece_q(outg, g), out_hbm.at[:, cols], o_r.at[g]).start()

        return carry

    lax.fori_loop(0, NX, block, 0)

    def deltas(i, carry):
        for cc in range(NC):
            grp = i * NC + cc
            if COMM:
                wait_group(functools.partial(piece_q, dog), do_r, grp)
            else:
                pl.when(grp == g)(lambda: wait_group(functools.partial(piece_q, dog), do_r, g))
        eye = iota((HD, HD), 0) == iota((HD, HD), 1)
        for h in range(REP):
            cols = pl.ds(h * HD, HD)
            grad = dog[pl.ds(i * BLK, BLK), cols]
            do4[i, pl.ds(h * BLK, BLK), :] = grad
            prod = grad.astype(jnp.float32) * outg[pl.ds(i * BLK, BLK), cols].astype(jnp.float32)
            total = jnp.broadcast_to(jnp.sum(prod, axis=1, keepdims=True), prod.shape)
            for t in range(BLK // HD):
                part = jnp.where(eye, total[t * HD : (t + 1) * HD], 0.0)
                del_row[i, :, pl.ds(h * BLK + t * HD, HD)] = jnp.sum(part, axis=0, keepdims=True)
        return carry

    lax.fori_loop(0, NX, deltas, 0)

    own = iota((256, 1), 0)

    def back(cp, carry):
        at = pl.ds(pl.multiple_of(cp * 256, 256), 256)
        rel = own + cp * 256 - c * BSP
        place = (rel % 32 // 8) * STEP + (rel // 32) * BLK + (rel % 8) * 32 + 31
        place = jnp.where(rel < 0, -1, jnp.where(rel >= BSP, LOC, place))
        dk_acc[...] = jnp.zeros((256, HD), jnp.float32)
        dv_acc[...] = jnp.zeros((256, HD), jnp.float32)

        def one(i, cr):
            keys, vals = kvb[at, pl.ds(0, HD)], kvb[at, pl.ds(HD, HD)]
            qs, gs = q4[i], do4[i]
            s = dot_t(keys, qs)
            here = iota((1, ROWS), 1) % BLK + i * STEP + z * BLK
            p = jnp.where(place <= here, jnp.exp2(s * C2 - lse_row[i]), 0.0)
            dp = dot_t(vals, gs)
            ds = (p * (dp - del_row[i])).astype(jnp.bfloat16)
            dv_acc[...] += dot_n(p.astype(jnp.bfloat16), gs)
            dk_acc[...] += dot_n(ds, qs)
            return cr

        lax.fori_loop(0, NX, one, 0)
        for a in range(2):
            for zz in range(NZ):
                s = (cp * 2 + a) * NZ + zz
                rows = pl.ds(a * BSP + zz * BEA, BEA)
                gacc[s, pl.ds(0, BEA), :] = dk_acc[rows, :] * SCALE
                gacc[s, pl.ds(BEA, BEA), :] = dv_acc[rows, :]
        if COMM:
            plane(cp * 2 * NZ, jnp.minimum(cp * 2 + 2, c + 1) * NZ, lambda s: g_send(s).start())
        return carry

    if BWD:
        lax.fori_loop(0, (c + 2) // 2, back, 0)

        row = iota((HD, 1), 0)
        dest, head, num = row // 16, (row // 4) % 4, row % 4
        spot = head * BLK + (dest % NC) * TOK + num * 32 + 31
        here = (dest // NC) * STEP + z * BLK + (dest % NC) * TOK + num * 32 + 31
        qb = jnp.zeros((HD, HD), jnp.float32)
        gb = jnp.zeros((HD, HD), jnp.float32)
        lse_b = jnp.zeros((HD, 1), jnp.float32)
        del_b = jnp.zeros((HD, 1), jnp.float32)
        for i in range(NX):
            pick = (iota((HD, ROWS), 1) == spot) & (dest // NC == i)
            hot = pick.astype(jnp.bfloat16)
            qb = qb + dot_n(hot, q4[i])
            gb = gb + dot_n(hot, do4[i])
            lse_b = lse_b + jnp.sum(jnp.where(pick, lse_row[i], 0.0), axis=1, keepdims=True)
            del_b = del_b + jnp.sum(jnp.where(pick, del_row[i], 0.0), axis=1, keepdims=True)
        qb = qb.astype(jnp.bfloat16)
        gb = gb.astype(jnp.bfloat16)

        def dq_part(keys, vals, seen):
            s = dot_t(qb, keys)
            p = jnp.where(seen(iota(s.shape, 1)), jnp.exp2(s * C2 - lse_b), 0.0)
            ds = (p * (dot_t(gb, vals) - del_b)).astype(jnp.bfloat16)
            return dot_n(ds, keys)

        def dq_prior(jp, total):
            at = pl.ds(pl.multiple_of(jp * 256, 256), 256)
            seen = lambda col: col < c * BSP - jp * 256
            return total + dq_part(kvb[at, pl.ds(0, HD)], kvb[at, pl.ds(HD, HD)], seen)

        dq = lax.fori_loop(0, n_prior, dq_prior, jnp.zeros((HD, HD), jnp.float32))

        def dq_local(j, total):
            at = pl.ds(pl.multiple_of(j * STEP, STEP), STEP)
            seen = lambda col: col + j * STEP <= here
            return total + dq_part(kv[at, pl.ds(0, HD)], kv[at, pl.ds(HD, HD)], seen)

        dq = lax.fori_loop(0, NX, dq_local, dq)
        dq_st[...] = dq * SCALE
    mine_rows = pl.ds(pl.multiple_of(g * 16, 16), 16)
    gq_in[mine_rows, :] = dq_st[mine_rows, :]
    if COMM:
        others(lambda grp: d_send(grp).start())

    dk_acc[pl.ds(0, 2 * BEA), :] = gacc[me]
    if COMM:

        def add(s):
            arrived(slots.at[s], g_r.at[s])
            dk_acc[pl.ds(0, 2 * BEA), :] += slots[s]

        plane(c * NZ, PLANE, add)
    for d in range(NG):
        tiles[d, pl.ds(0, 4), :] = dk_acc[pl.ds(d * 4, 4), :]
        tiles[d, pl.ds(4, 4), :] = dk_acc[pl.ds(BEA + d * 4, 4), :]
    gkv_in[g] = tiles[g]
    if COMM:
        others(lambda grp: t_send(grp).start())
        others(lambda grp: arrived(gq_in.at[pl.ds(pl.multiple_of(grp * 16, 16), 16), :], d_r.at[grp]))
        others(lambda grp: arrived(gkv_in.at[grp], t_r.at[grp]))
    for grp in range(NG):
        gk_ref[:, pl.ds(grp * HD, HD)] = gkv_in[grp, pl.ds(0, 4), :]
        gv_ref[:, pl.ds(grp * HD, HD)] = gkv_in[grp, pl.ds(4, 4), :]
        for h in range(REP):
            gq_ref[:, pl.ds((grp * REP + h) * HD, HD)] = gq_in[pl.ds(grp * 16 + h * 4, 4), :]

    def out_cols(grp):
        return out_hbm.at[:, pl.ds(pl.multiple_of(grp * REP * HD, REP * HD), REP * HD)]

    if FWD:
        arrived(out_cols(g), o_r.at[g])
    if COMM:
        others(lambda grp: arrived(out_cols(grp), o_r.at[grp]))
        for which in range(4):
            others(lambda grp, which=which: remote(*x_copies(grp)[which], in_group(grp)).wait_send())
        for xx in range(NX):
            for way in range(2):
                z_send(xx, way).wait_send()
                z_relay(xx, way).wait_send()
        plane(c * NZ, PLANE, lambda s: b_send(s).wait_send())
        others(lambda grp: o_send(grp).wait_send())
        plane(0, (c + 1) * NZ, lambda s: g_send(s).wait_send())
        others(lambda grp: d_send(grp).wait_send())
        others(lambda grp: t_send(grp).wait_send())


def on_device(query, key, value, d_out):
    f32, b16 = jnp.float32, jnp.bfloat16
    vm = pltpu.VMEM
    dma = pltpu.SemaphoreType.DMA
    scratch = [
        vm((LOC, 3 * HD), b16), vm((ALLB, 3 * HD), b16), vm((BEA, 2 * HD), b16),
        vm((NX * BLK, REP * HD), b16), vm((NX * BLK, REP * HD), b16), vm((NX * BLK, REP * HD), b16),
        vm((NX, ROWS, HD), b16), vm((NX, ROWS, HD), b16),
        vm((1 + NX, ROWS, STEP), f32), vm((ROWS, HD), f32), vm((ROWS, 2 * HD), f32),
        vm((NX, 1, ROWS), f32), vm((NX, 1, ROWS), f32),
        vm((256, HD), f32), vm((256, HD), f32), vm((PLANE, 2 * BEA, HD), f32), vm((PLANE, 2 * BEA, HD), f32),
        vm((NG, 8, HD), f32), vm((NG, 8, HD), f32), vm((HD, HD), f32), vm((HD, HD), f32),
        dma((NG,)), dma((NG,)), dma((NG,)), dma((NG,)), dma((NG,)), dma((NG,)), dma((NG,)), dma((NG,)),
        dma((NX, 2)), dma((NX, 4)), dma((NX, 2)), dma((PLANE,)), dma((PLANE,)),
        dma((NG,)), dma((NG,)), dma((PLANE,)), dma((PLANE,)), dma((NG,)), dma((NG,)), dma((NG,)), dma((NG,)),
    ]
    anyspace = pl.BlockSpec(memory_space=pl.ANY)
    inner = pl.BlockSpec(memory_space=pltpu.VMEM)
    return pl.pallas_call(
        fused,
        out_shape=(
            jax.ShapeDtypeStruct((TOK, NG * REP * HD), b16),
            jax.ShapeDtypeStruct((4, NG * REP * HD), f32),
            jax.ShapeDtypeStruct((4, NG * HD), f32),
            jax.ShapeDtypeStruct((4, NG * HD), f32),
        ),
        in_specs=[anyspace] * 4,
        out_specs=(anyspace, inner, inner, inner),
        scratch_shapes=scratch,
        compiler_params=pltpu.CompilerParams(
            collective_id=0 if COMM else None, has_side_effects=True, vmem_limit_bytes=60 * 1024 * 1024
        ),
    )(query, key, value, d_out)


def solution(mesh):
    spec = P(("span", "ulysses"), None)
    return jax.shard_map(
        on_device, mesh=mesh, in_specs=(spec,) * 4, out_specs=(spec,) * 4, check_vma=False
    )
```

time: 741 us -> 121 us (0.16); the launches traced: 729 us -> 121 us
  local copies, waits for them, and re-layouts: 236 us -> 4.37 us
  matrix products: 165 us -> 0 us
  Pallas kernels: 0 us -> 116 us
  waiting for transfers between devices: 92.1 us -> 0 us
  other arithmetic: 77.3 us -> 0 us
  starting transfers between devices: 71.2 us -> 0 us
  blocking collectives: 70.7 us -> 0 us
  between operations: 16.1 us -> 0.65 us
    dot_general x88 -> x0, matrix products: 165 us -> none  [the longest x8 24.8 us: on_device(): jnp.einsum('hqk,khd->qhd', b_local, v_loc, preferred_element_type=jnp.flo...]
    pallas_call x0 -> x1, Pallas kernels: none -> 116 us  [on_device(): pl.pallas_call(fused, out_shape=(jax.ShapeDtypeStruct((TOK, NG * REP * HD...]
    slice x93 -> x0, local copies, waits for them, and re-layouts: 115 us -> none  [the longest x8 16.7 us: on_device(): p_rows_local = p_local.reshape(per_dev, n_rows, INTERVAL, upper)[:, :, -1]]
    all_to_all x8 -> x0, waiting for transfers between devices: 92 us -> none  [the longest x1 29.3 us: on_device(): lax.all_to_all(widen(value), 'ulysses', split_axis=1, concat_axis=0, tile...]
    all_to_all x8 -> x0, starting transfers between devices: 71.2 us -> none  [the longest x1 17 us: on_device(): lax.all_to_all(grad_q_heads, 'ulysses', split_axis=0, concat_axis=1, tile...]
    all_gather x2 -> x0, blocking collectives: 70.7 us -> none  [the longest x1 37.2 us: on_device(): lax.all_gather(own_k, 'span', axis=0, tiled=True)]
    div x8 -> x0, local copies, waits for them, and re-layouts: 45.1 us -> none  [on_device(): p_local = e_local / denom[:, :, None]]
    convert_element_type x15 -> x0, local copies, waits for them, and re-layouts: 44.8 us -> none  [the longest x7 30.5 us: on_device(): b_local = p_local.astype(jnp.bfloat16)]
  transfers between devices with their start and end apart: 9 -> 0, of which waited for: 5 -> 0; matrix products, arithmetic and copies ran while one was open for 15% -> 0% of each run, Pallas kernels for 0% -> 0%
where the time goes in v1:
time: 121 us
  Pallas kernels  116 us (96%)
  local copies, waits for them, and re-layouts  4.37 us (4%)
    pallas_call x1, Pallas kernels, on_device(): pl.pallas_call(fused, out_shape=(jax.ShapeDtypeStruct((TOK, NG * REP * HD...  116 us
    unnamed x10, local copies, waits for them, and re-layouts  4.37 us

profile of v1, /device:TPU:57, one launch (start us, length us, event | category | flops | bytes accessed | tf_op | source)
XLA Modules:
  0.0 121.2 jit_solution(8983012106469888656)
XLA Ops:
  0.6 116.1 %shard_map.75 = (bf16[128,4096]{1,0:T(8,128)(2,1)}, f32[4,4096]{1,0:T(4,128)}, f32[4,1024]{1,0:T(4,128)}, f32[4,1024]{1,0:T(4,128)}) custom-call(bf16[128,4096]{1,0:T(8,128)(2,1)} %q_hbm.1, bf16[128,1024]{1,0:T(8,128)(2,1)} %k_hbm.1, bf16[128,1024]{1,0:T(8,128)(2,1)} %v_hbm.1, bf16[128,4096]{1,0:T(8,128)(2,1)} %do_hbm.1), custom_call_target="tpu_custom_call" | custom-call | tf_op jit(solution)/shard_map/pallas_call | solution.py:473
  116.8 0.0 copy-start
  116.8 2.3 %copy.12 = bf16[128,4096]{1,0:T(8,128)(2,1)} copy(bf16[128,4096]{1,0:T(8,128)(2,1)} %get-tuple-element.8) | data formatting | bytes 2097152
  119.1 0.0 copy-done
  119.1 0.0 copy-start.2
  119.1 0.6 copy.13
  119.7 0.1 copy-done.2
  119.8 0.0 copy-start.1
  119.8 0.6 copy.14
  120.4 0.1 copy-done.1
  120.5 0.6 copy.15
Async XLA Ops:
  116.8 2.3 %copy-start = (f32[4,4096]{1,0:T(4,128)S(1)}, f32[4,4096]{1,0:T(4,128)}, u32[]{:S(2)}) copy-start(f32[4,4096]{1,0:T(4,128)} %get-tuple-element.9) | copy-start | bytes 196612
  119.1 0.7 copy-start.2
  119.8 0.7 copy-start.1

commit v2 on v1

--- a/solution.py
+++ b/solution.py
@@ -173,16 +173,29 @@
     def wait_group(buf_piece, sem, grp):
         arrived(buf_piece(grp), sem.at[grp])
 
-    for xx in range(NX):
+    def kv_here(xx):
         for cc in range(NC):
-            grp = xx * NC + cc
-            if COMM:
-                wait_group(piece_k, kx_r, grp)
-                wait_group(piece_v, vx_r, grp)
-        if COMM:
-            z_send(xx, 0).start()
-            z_send(xx, 1).start()
-    if not COMM:
+            wait_group(piece_k, kx_r, xx * NC + cc)
+            wait_group(piece_v, vx_r, xx * NC + cc)
+
+    def z_direct(xx):
+        z_send(xx, 0).start()
+        z_send(xx, 1).start()
+
+    def z_pass_on(xx):
+        arrived(z_piece(xx, zm, 0, 2 * HD), z_r.at[xx, 0])
+        z_relay(xx, 0).start()
+        arrived(z_piece(xx, zp, 0, 2 * HD), z_r.at[xx, 1])
+        z_relay(xx, 1).start()
+
+    if COMM:
+        kv_here(0)
+        z_direct(0)
+        kv_here(1)
+        z_direct(1)
+        kv_here(2)
+        kv_here(3)
+    else:
         wait_group(piece_k, kx_r, g)
         wait_group(piece_v, vx_r, g)
 
@@ -193,32 +206,37 @@
         picked = picked + dot_n(hot, kv[z_rows(xx, z), pl.ds(0, 2 * HD)])
     bst[...] = picked.astype(jnp.bfloat16)
     kvb[pl.ds(pl.multiple_of(me * BEA, BEA), BEA), pl.ds(0, 2 * HD)] = bst[...]
+    dk_acc[...] = jnp.zeros((ALLB, HD), jnp.float32)
+    dv_acc[...] = jnp.zeros((ALLB, HD), jnp.float32)
+    n_prior = (c + 1) // 2
+    n_back = (c + 2) // 2
+    z2 = (z + 2) % NZ
     if COMM:
         plane(c * NZ, PLANE, lambda s: b_send(s).start())
-        for xx in range(NX):
-            arrived(z_piece(xx, zm, 0, 2 * HD), z_r.at[xx, 0])
-            z_relay(xx, 0).start()
-            arrived(z_piece(xx, zp, 0, 2 * HD), z_r.at[xx, 1])
-            z_relay(xx, 1).start()
+        z_pass_on(0)
+        z_direct(2)
+        z_pass_on(1)
+        z_direct(3)
         plane(0, (c + 1) * NZ, lambda s: arrived(b_rows(s), b_r.at[s]))
 
-    n_prior = (c + 1) // 2
-    z2 = (z + 2) % NZ
+    own = iota((256, 1), 0)
 
     def block(i, carry):
+        if COMM:
+            @pl.when((i == 1) | (i == 2))
+            def _():
+                z_pass_on(i + 1)
+
+            arrived(z_piece(i, z2, 0, HD), z_r.at[i, 2])
+            arrived(z_piece(i, z2, HD, HD), z_r.at[i, 3])
         for cc in range(NC):
             grp = i * NC + cc
             if COMM:
                 wait_group(functools.partial(piece_q, qg), q_r, grp)
             else:
                 pl.when(grp == g)(lambda: wait_group(functools.partial(piece_q, qg), q_r, g))
-        if COMM:
-            arrived(z_piece(i, z2, 0, HD), z_r.at[i, 2])
-            arrived(z_piece(i, z2, HD, HD), z_r.at[i, 3])
         for h in range(REP):
             q4[i, pl.ds(h * BLK, BLK), :] = qg[pl.ds(i * BLK, BLK), pl.ds(h * HD, HD)]
-        if not FWD:
-            return carry
         mx[...] = jnp.full((ROWS, HD), -jnp.inf, jnp.float32)
 
         def widest(s, rows):
@@ -306,11 +324,6 @@
                 cols = pl.ds(pl.multiple_of(g * REP * HD, REP * HD), REP * HD)
                 pltpu.make_async_copy(piece_q(outg, g), out_hbm.at[:, cols], o_r.at[g]).start()
 
-        return carry
-
-    lax.fori_loop(0, NX, block, 0)
-
-    def deltas(i, carry):
         for cc in range(NC):
             grp = i * NC + cc
             if COMM:
@@ -327,46 +340,39 @@
             for t in range(BLK // HD):
                 part = jnp.where(eye, total[t * HD : (t + 1) * HD], 0.0)
                 del_row[i, :, pl.ds(h * BLK + t * HD, HD)] = jnp.sum(part, axis=0, keepdims=True)
+
+        def back(cp, cr):
+            at = pl.ds(pl.multiple_of(cp * 256, 256), 256)
+            rel = own + cp * 256 - c * BSP
+            place = (rel % 32 // 8) * STEP + (rel // 32) * BLK + (rel % 8) * 32 + 31
+            place = jnp.where(rel < 0, -1, jnp.where(rel >= BSP, LOC, place))
+            keys, vals = kvb[at, pl.ds(0, HD)], kvb[at, pl.ds(HD, HD)]
+            here = iota((1, ROWS), 1) % BLK + i * STEP + z * BLK
+            p = jnp.where(place <= here, jnp.exp2(dot_t(keys, q4[i]) * C2 - lse_row[i]), 0.0)
+            dp = dot_t(vals, do4[i])
+            ds = (p * (dp - del_row[i])).astype(jnp.bfloat16)
+            dv_acc[at, :] += dot_n(p.astype(jnp.bfloat16), do4[i])
+            dk_acc[at, :] += dot_n(ds, q4[i])
+
+            @pl.when(i == NX - 1)
+            def _():
+                for a in range(2):
+                    for zz in range(NZ):
+                        s = (cp * 2 + a) * NZ + zz
+                        rows = pl.ds(pl.multiple_of(s * BEA, BEA), BEA)
+                        gacc[s, pl.ds(0, BEA), :] = dk_acc[rows, :] * SCALE
+                        gacc[s, pl.ds(BEA, BEA), :] = dv_acc[rows, :]
+                if COMM:
+                    plane(cp * 2 * NZ, jnp.minimum(cp * 2 + 2, c + 1) * NZ, lambda s: g_send(s).start())
+
+            return cr
+
+        if BWD:
+            lax.fori_loop(0, n_back, back, 0)
         return carry
 
-    lax.fori_loop(0, NX, deltas, 0)
-
-    own = iota((256, 1), 0)
-
-    def back(cp, carry):
-        at = pl.ds(pl.multiple_of(cp * 256, 256), 256)
-        rel = own + cp * 256 - c * BSP
-        place = (rel % 32 // 8) * STEP + (rel // 32) * BLK + (rel % 8) * 32 + 31
-        place = jnp.where(rel < 0, -1, jnp.where(rel >= BSP, LOC, place))
-        dk_acc[...] = jnp.zeros((256, HD), jnp.float32)
-        dv_acc[...] = jnp.zeros((256, HD), jnp.float32)
-
-        def one(i, cr):
-            keys, vals = kvb[at, pl.ds(0, HD)], kvb[at, pl.ds(HD, HD)]
-            qs, gs = q4[i], do4[i]
-            s = dot_t(keys, qs)
-            here = iota((1, ROWS), 1) % BLK + i * STEP + z * BLK
-            p = jnp.where(place <= here, jnp.exp2(s * C2 - lse_row[i]), 0.0)
-            dp = dot_t(vals, gs)
-            ds = (p * (dp - del_row[i])).astype(jnp.bfloat16)
-            dv_acc[...] += dot_n(p.astype(jnp.bfloat16), gs)
-            dk_acc[...] += dot_n(ds, qs)
-            return cr
-
-        lax.fori_loop(0, NX, one, 0)
-        for a in range(2):
-            for zz in range(NZ):
-                s = (cp * 2 + a) * NZ + zz
-                rows = pl.ds(a * BSP + zz * BEA, BEA)
-                gacc[s, pl.ds(0, BEA), :] = dk_acc[rows, :] * SCALE
-                gacc[s, pl.ds(BEA, BEA), :] = dv_acc[rows, :]
-        if COMM:
-            plane(cp * 2 * NZ, jnp.minimum(cp * 2 + 2, c + 1) * NZ, lambda s: g_send(s).start())
-        return carry
-
+    lax.fori_loop(0, NX, block, 0)
     if BWD:
-        lax.fori_loop(0, (c + 2) // 2, back, 0)
-
         row = iota((HD, 1), 0)
         dest, head, num = row // 16, (row // 4) % 4, row % 4
         spot = head * BLK + (dest % NC) * TOK + num * 32 + 31
@@ -462,7 +468,7 @@
         vm((NX, ROWS, HD), b16), vm((NX, ROWS, HD), b16),
         vm((1 + NX, ROWS, STEP), f32), vm((ROWS, HD), f32), vm((ROWS, 2 * HD), f32),
         vm((NX, 1, ROWS), f32), vm((NX, 1, ROWS), f32),
-        vm((256, HD), f32), vm((256, HD), f32), vm((PLANE, 2 * BEA, HD), f32), vm((PLANE, 2 * BEA, HD), f32),
+        vm((ALLB, HD), f32), vm((ALLB, HD), f32), vm((PLANE, 2 * BEA, HD), f32), vm((PLANE, 2 * BEA, HD), f32),
         vm((NG, 8, HD), f32), vm((NG, 8, HD), f32), vm((HD, HD), f32), vm((HD, HD), f32),
         dma((NG,)), dma((NG,)), dma((NG,)), dma((NG,)), dma((NG,)), dma((NG,)), dma((NG,)), dma((NG,)),
         dma((NX, 2)), dma((NX, 4)), dma((NX, 2)), dma((PLANE,)), dma((PLANE,)),

time: 121 us -> 121 us (level)
  no operation moved by 1% of the time
where the time goes in v2:
time: 121 us
  Pallas kernels  116 us (96%)
  local copies, waits for them, and re-layouts  4.37 us (4%)
    pallas_call x1, Pallas kernels, on_device(): pl.pallas_call(fused, out_shape=(jax.ShapeDtypeStruct((TOK, NG * REP * HD...  116 us
    unnamed x10, local copies, waits for them, and re-layouts  4.37 us

profile of v2, /device:TPU:57, one launch (start us, length us, event | category | flops | bytes accessed | tf_op | source)
XLA Modules:
  0.0 121.2 jit_solution(7873976246641243061)
XLA Ops:
  0.6 116.2 %shard_map.75 = (bf16[128,4096]{1,0:T(8,128)(2,1)}, f32[4,4096]{1,0:T(4,128)}, f32[4,1024]{1,0:T(4,128)}, f32[4,1024]{1,0:T(4,128)}) custom-call(bf16[128,4096]{1,0:T(8,128)(2,1)} %q_hbm.1, bf16[128,1024]{1,0:T(8,128)(2,1)} %k_hbm.1, bf16[128,1024]{1,0:T(8,128)(2,1)} %v_hbm.1, bf16[128,4096]{1,0:T(8,128)(2,1)} %do_hbm.1), custom_call_target="tpu_custom_call" | custom-call | tf_op jit(solution)/shard_map/pallas_call | solution.py:479
  116.8 0.0 copy-start
  116.8 2.3 %copy.12 = bf16[128,4096]{1,0:T(8,128)(2,1)} copy(bf16[128,4096]{1,0:T(8,128)(2,1)} %get-tuple-element.8) | data formatting | bytes 2097152
  119.2 0.0 copy-done
  119.2 0.0 copy-start.2
  119.2 0.6 copy.13
  119.8 0.1 copy-done.2
  119.9 0.0 copy-start.1
  119.9 0.6 copy.14
  120.5 0.1 copy-done.1
  120.6 0.6 copy.15
Async XLA Ops:
  116.8 2.3 %copy-start = (f32[4,4096]{1,0:T(4,128)S(1)}, f32[4,4096]{1,0:T(4,128)}, u32[]{:S(2)}) copy-start(f32[4,4096]{1,0:T(4,128)} %get-tuple-element.9) | copy-start | bytes 196612
  119.2 0.7 copy-start.2
  119.9 0.7 copy-start.1

commit v3 on v2

--- a/solution.py
+++ b/solution.py
@@ -46,7 +46,7 @@
     q_hbm, k_hbm, v_hbm, do_hbm,
     out_hbm, gq_ref, gk_ref, gv_ref,
     kv, kvb, bst, qg, dog, outg, q4, do4, sbuf, mx, acc, lse_row, del_row,
-    dk_acc, dv_acc, gacc, slots, tiles, gkv_in, dq_st, gq_in,
+    dk_acc, dv_acc, pb, dsb, gown, gacc, slots, tiles, gkv_in, dq_st, gq_in,
     kx_s, kx_r, vx_s, vx_r, q_s, q_r, do_s, do_r, z_s, z_r, zr_s, b_s, b_r,
     o_s, o_r, g_s, g_r, t_s, t_r, d_s, d_r,
 ):
@@ -206,8 +206,6 @@
         picked = picked + dot_n(hot, kv[z_rows(xx, z), pl.ds(0, 2 * HD)])
     bst[...] = picked.astype(jnp.bfloat16)
     kvb[pl.ds(pl.multiple_of(me * BEA, BEA), BEA), pl.ds(0, 2 * HD)] = bst[...]
-    dk_acc[...] = jnp.zeros((ALLB, HD), jnp.float32)
-    dv_acc[...] = jnp.zeros((ALLB, HD), jnp.float32)
     n_prior = (c + 1) // 2
     n_back = (c + 2) // 2
     z2 = (z + 2) % NZ
@@ -341,38 +339,51 @@
                 part = jnp.where(eye, total[t * HD : (t + 1) * HD], 0.0)
                 del_row[i, :, pl.ds(h * BLK + t * HD, HD)] = jnp.sum(part, axis=0, keepdims=True)
 
-        def back(cp, cr):
-            at = pl.ds(pl.multiple_of(cp * 256, 256), 256)
-            rel = own + cp * 256 - c * BSP
-            place = (rel % 32 // 8) * STEP + (rel // 32) * BLK + (rel % 8) * 32 + 31
-            place = jnp.where(rel < 0, -1, jnp.where(rel >= BSP, LOC, place))
-            keys, vals = kvb[at, pl.ds(0, HD)], kvb[at, pl.ds(HD, HD)]
-            here = iota((1, ROWS), 1) % BLK + i * STEP + z * BLK
-            p = jnp.where(place <= here, jnp.exp2(dot_t(keys, q4[i]) * C2 - lse_row[i]), 0.0)
-            dp = dot_t(vals, do4[i])
-            ds = (p * (dp - del_row[i])).astype(jnp.bfloat16)
-            dv_acc[at, :] += dot_n(p.astype(jnp.bfloat16), do4[i])
-            dk_acc[at, :] += dot_n(ds, q4[i])
-
-            @pl.when(i == NX - 1)
-            def _():
-                for a in range(2):
-                    for zz in range(NZ):
-                        s = (cp * 2 + a) * NZ + zz
-                        rows = pl.ds(pl.multiple_of(s * BEA, BEA), BEA)
-                        gacc[s, pl.ds(0, BEA), :] = dk_acc[rows, :] * SCALE
-                        gacc[s, pl.ds(BEA, BEA), :] = dv_acc[rows, :]
-                if COMM:
-                    plane(cp * 2 * NZ, jnp.minimum(cp * 2 + 2, c + 1) * NZ, lambda s: g_send(s).start())
-
+        return carry
+
+    lax.fori_loop(0, NX, block, 0)
+
+    def back(cp, carry):
+        at = pl.ds(pl.multiple_of(cp * 256, 256), 256)
+        rel = own + cp * 256 - c * BSP
+        place = (rel % 32 // 8) * STEP + (rel // 32) * BLK + (rel % 8) * 32 + 31
+        place = jnp.where(rel < 0, -1, jnp.where(rel >= BSP, LOC, place))
+        keys, vals = kvb[at, pl.ds(0, HD)], kvb[at, pl.ds(HD, HD)]
+        dk_acc[...] = jnp.zeros((256, HD), jnp.float32)
+        dv_acc[...] = jnp.zeros((256, HD), jnp.float32)
+
+        def one(i, cr):
+            for h in range(REP):
+                rows = pl.ds(h * BLK, BLK)
+                qs, gs = q4[i, rows, :], do4[i, rows, :]
+                here = iota((1, BLK), 1) + i * STEP + z * BLK
+                p = jnp.where(place <= here, jnp.exp2(dot_t(keys, qs) * C2 - lse_row[i, :, rows]), 0.0)
+                dsb[:, rows] = (p * (dot_t(vals, gs) - del_row[i, :, rows])).astype(jnp.bfloat16)
+                pb[:, rows] = p.astype(jnp.bfloat16)
+            dv_acc[...] += dot_n(pb[...], do4[i])
+            dk_acc[...] += dot_n(dsb[...], q4[i])
             return cr
 
-        if BWD:
-            lax.fori_loop(0, n_back, back, 0)
+        lax.fori_loop(0, NX, one, 0)
+        for a in range(2):
+            for zz in range(NZ):
+                s = (cp * 2 + a) * NZ + zz
+                rows = pl.ds(a * BSP + zz * BEA, BEA)
+                gacc[s, pl.ds(0, BEA), :] = (dk_acc[rows, :] * SCALE).astype(jnp.bfloat16)
+                gacc[s, pl.ds(BEA, BEA), :] = dv_acc[rows, :].astype(jnp.bfloat16)
+
+                @pl.when(s == me)
+                def _():
+                    gown[pl.ds(0, BEA), :] = dk_acc[rows, :] * SCALE
+                    gown[pl.ds(BEA, BEA), :] = dv_acc[rows, :]
+
+        if COMM:
+            plane(cp * 2 * NZ, jnp.minimum(cp * 2 + 2, c + 1) * NZ, lambda s: g_send(s).start())
         return carry
 
-    lax.fori_loop(0, NX, block, 0)
     if BWD:
+        lax.fori_loop(0, n_back, back, 0)
+
         row = iota((HD, 1), 0)
         dest, head, num = row // 16, (row // 4) % 4, row % 4
         spot = head * BLK + (dest % NC) * TOK + num * 32 + 31
@@ -416,17 +427,16 @@
     if COMM:
         others(lambda grp: d_send(grp).start())
 
-    dk_acc[pl.ds(0, 2 * BEA), :] = gacc[me]
     if COMM:
 
         def add(s):
             arrived(slots.at[s], g_r.at[s])
-            dk_acc[pl.ds(0, 2 * BEA), :] += slots[s]
+            gown[...] += slots[s].astype(jnp.float32)
 
         plane(c * NZ, PLANE, add)
     for d in range(NG):
-        tiles[d, pl.ds(0, 4), :] = dk_acc[pl.ds(d * 4, 4), :]
-        tiles[d, pl.ds(4, 4), :] = dk_acc[pl.ds(BEA + d * 4, 4), :]
+        tiles[d, pl.ds(0, 4), :] = gown[pl.ds(d * 4, 4), :]
+        tiles[d, pl.ds(4, 4), :] = gown[pl.ds(BEA + d * 4, 4), :]
     gkv_in[g] = tiles[g]
     if COMM:
         others(lambda grp: t_send(grp).start())
@@ -468,7 +478,7 @@
         vm((NX, ROWS, HD), b16), vm((NX, ROWS, HD), b16),
         vm((1 + NX, ROWS, STEP), f32), vm((ROWS, HD), f32), vm((ROWS, 2 * HD), f32),
         vm((NX, 1, ROWS), f32), vm((NX, 1, ROWS), f32),
-        vm((ALLB, HD), f32), vm((ALLB, HD), f32), vm((PLANE, 2 * BEA, HD), f32), vm((PLANE, 2 * BEA, HD), f32),
+        vm((256, HD), f32), vm((256, HD), f32), vm((256, ROWS), b16), vm((256, ROWS), b16), vm((2 * BEA, HD), f32), vm((PLANE, 2 * BEA, HD), b16), vm((PLANE, 2 * BEA, HD), b16),
         vm((NG, 8, HD), f32), vm((NG, 8, HD), f32), vm((HD, HD), f32), vm((HD, HD), f32),
         dma((NG,)), dma((NG,)), dma((NG,)), dma((NG,)), dma((NG,)), dma((NG,)), dma((NG,)), dma((NG,)),
         dma((NX, 2)), dma((NX, 4)), dma((NX, 2)), dma((PLANE,)), dma((PLANE,)),

time: 121 us -> 113 us (0.934)
  Pallas kernels: 116 us -> 108 us
    pallas_call x1, Pallas kernels: 116 us -> 108 us  [on_device(): pl.pallas_call(fused, out_shape=(jax.ShapeDtypeStruct((TOK, NG * REP * HD...]
where the time goes in v3:
time: 113 us
  Pallas kernels  108 us (96%)
  local copies, waits for them, and re-layouts  4.37 us (4%)
    pallas_call x1, Pallas kernels, on_device(): pl.pallas_call(fused, out_shape=(jax.ShapeDtypeStruct((TOK, NG * REP * HD...  108 us
    unnamed x10, local copies, waits for them, and re-layouts  4.37 us

profile of v3, /device:TPU:57, one launch (start us, length us, event | category | flops | bytes accessed | tf_op | source)
XLA Modules:
  0.0 112.9 jit_solution(5706736451181669159)
XLA Ops:
  0.6 107.9 %shard_map.75 = (bf16[128,4096]{1,0:T(8,128)(2,1)}, f32[4,4096]{1,0:T(4,128)}, f32[4,1024]{1,0:T(4,128)}, f32[4,1024]{1,0:T(4,128)}) custom-call(bf16[128,4096]{1,0:T(8,128)(2,1)} %q_hbm.1, bf16[128,1024]{1,0:T(8,128)(2,1)} %k_hbm.1, bf16[128,1024]{1,0:T(8,128)(2,1)} %v_hbm.1, bf16[128,4096]{1,0:T(8,128)(2,1)} %do_hbm.1), custom_call_target="tpu_custom_call" | custom-call | tf_op jit(solution)/shard_map/pallas_call | solution.py:489
  108.6 0.0 copy-start
  108.6 2.3 %copy.12 = bf16[128,4096]{1,0:T(8,128)(2,1)} copy(bf16[128,4096]{1,0:T(8,128)(2,1)} %get-tuple-element.8) | data formatting | bytes 2097152
  110.9 0.0 copy-done
  110.9 0.0 copy-start.2
  110.9 0.6 copy.13
  111.5 0.1 copy-done.2
  111.6 0.0 copy-start.1
  111.6 0.6 copy.14
  112.2 0.1 copy-done.1
  112.3 0.6 copy.15
Async XLA Ops:
  108.6 2.3 %copy-start = (f32[4,4096]{1,0:T(4,128)S(1)}, f32[4,4096]{1,0:T(4,128)}, u32[]{:S(2)}) copy-start(f32[4,4096]{1,0:T(4,128)} %get-tuple-element.9) | copy-start | bytes 196612
  110.9 0.7 copy-start.2
  111.6 0.7 copy-start.1

commit v4 on v3

--- a/solution.py
+++ b/solution.py
@@ -25,6 +25,7 @@
 LOG2E = 1.4426950408889634
 C2 = SCALE * LOG2E
 MESH = pl.DeviceIdType.MESH
+PCH = 1024
 COMM = True
 FWD = True
 BWD = True
@@ -207,6 +208,7 @@
     bst[...] = picked.astype(jnp.bfloat16)
     kvb[pl.ds(pl.multiple_of(me * BEA, BEA), BEA), pl.ds(0, 2 * HD)] = bst[...]
     n_prior = (c + 1) // 2
+    n_chunk = (c * BSP + PCH - 1) // PCH
     n_back = (c + 2) // 2
     z2 = (z + 2) % NZ
     if COMM:
@@ -218,6 +220,12 @@
         plane(0, (c + 1) * NZ, lambda s: arrived(b_rows(s), b_r.at[s]))
 
     own = iota((256, 1), 0)
+
+    def blank(s, carry):
+        kvb[pl.ds(pl.multiple_of(s * BSP, BSP), BSP), pl.ds(0, 2 * HD)] = jnp.zeros((BSP, 2 * HD), jnp.bfloat16)
+        return carry
+
+    lax.fori_loop(c + 1, NS, blank, 0)
 
     def block(i, carry):
         if COMM:
@@ -244,22 +252,22 @@
             mx[rows, :] = jnp.maximum(mx[rows, :], top)
 
         def score_prior(jp, cr):
-            keys = kvb[pl.ds(pl.multiple_of(jp * 256, 256), 256), pl.ds(0, HD)]
+            keys = kvb[pl.ds(pl.multiple_of(jp * PCH, PCH), PCH), pl.ds(0, HD)]
             for h in range(REP):
                 rows = pl.ds(h * BLK, BLK)
-                s = dot_t(q4[i, rows, :], keys)
-                s = jnp.where(iota(s.shape, 1) < c * BSP - jp * 256, s, -jnp.inf)
-                sbuf[0, rows, pl.ds(pl.multiple_of(jp * 256, 256), 256)] = s
+                s = dot_t(q4[i, rows, :], keys) * C2
+                s = jnp.where(iota(s.shape, 1) < c * BSP - jp * PCH, s, -jnp.inf)
+                sbuf[0, rows, pl.ds(pl.multiple_of(jp * PCH, PCH), PCH)] = s
                 widest(s, rows)
             return cr
 
-        lax.fori_loop(0, n_prior, score_prior, 0)
+        lax.fori_loop(0, n_chunk, score_prior, 0)
 
         def score(j, masked):
             keys = kv[pl.ds(pl.multiple_of(j * STEP, STEP), STEP), pl.ds(0, HD)]
             for h in range(REP):
                 rows = pl.ds(h * BLK, BLK)
-                s = dot_t(q4[i, rows, :], keys)
+                s = dot_t(q4[i, rows, :], keys) * C2
                 if masked:
                     s = jnp.where(iota(s.shape, 1) - iota(s.shape, 0) <= z * BLK, s, -jnp.inf)
                 sbuf[1 + j, rows, :] = s
@@ -272,25 +280,25 @@
         lax.fori_loop(0, i, score_full, 0)
         score(i, True)
 
-        peak = jnp.max(mx[...], axis=1, keepdims=True) * C2
+        peak = jnp.max(mx[...], axis=1, keepdims=True)
         mx[...] = jnp.broadcast_to(peak, (ROWS, HD))
         acc[...] = jnp.zeros((ROWS, 2 * HD), jnp.float32)
 
         def spread(s, rows):
             m = mx[rows, :]
             return jnp.concatenate(
-                [jnp.exp2(s[:, t * HD : (t + 1) * HD] * C2 - m) for t in range(s.shape[1] // HD)], axis=1
+                [jnp.exp2(s[:, t * HD : (t + 1) * HD] - m) for t in range(s.shape[1] // HD)], axis=1
             ).astype(jnp.bfloat16)
 
         def mix_prior(jp, cr):
-            at = pl.ds(pl.multiple_of(jp * 256, 256), 256)
+            at = pl.ds(pl.multiple_of(jp * PCH, PCH), PCH)
             vals = kvb[at, pl.ds(HD, 2 * HD)]
             for h in range(REP):
                 rows = pl.ds(h * BLK, BLK)
                 acc[rows, :] += dot_n(spread(sbuf[0, rows, at], rows), vals)
             return cr
 
-        lax.fori_loop(0, n_prior, mix_prior, 0)
+        lax.fori_loop(0, n_chunk, mix_prior, 0)
 
         def mix(j, cr):
             vals = kv[pl.ds(pl.multiple_of(j * STEP, STEP), STEP), pl.ds(HD, 2 * HD)]
@@ -322,6 +330,11 @@
                 cols = pl.ds(pl.multiple_of(g * REP * HD, REP * HD), REP * HD)
                 pltpu.make_async_copy(piece_q(outg, g), out_hbm.at[:, cols], o_r.at[g]).start()
 
+        return carry
+
+    lax.fori_loop(0, NX, block, 0)
+
+    def deltas(i, carry):
         for cc in range(NC):
             grp = i * NC + cc
             if COMM:
@@ -341,7 +354,7 @@
 
         return carry
 
-    lax.fori_loop(0, NX, block, 0)
+    lax.fori_loop(0, NX, deltas, 0)
 
     def back(cp, carry):
         at = pl.ds(pl.multiple_of(cp * 256, 256), 256)

time: 113 us -> 110 us (0.973)
  Pallas kernels: 108 us -> 104 us
    pallas_call x1, Pallas kernels: 108 us -> 104 us  [on_device(): pl.pallas_call(fused, out_shape=(jax.ShapeDtypeStruct((TOK, NG * REP * HD...]
where the time goes in v4:
time: 110 us; the launch traced here: 109 us
  Pallas kernels  104 us (95%)
  local copies, waits for them, and re-layouts  4.37 us (4%)
    pallas_call x1, Pallas kernels, on_device(): pl.pallas_call(fused, out_shape=(jax.ShapeDtypeStruct((TOK, NG * REP * HD...  104 us
    unnamed x10, local copies, waits for them, and re-layouts  4.37 us

profile of v4, /device:TPU:57, one launch (start us, length us, event | category | flops | bytes accessed | tf_op | source)
XLA Modules:
  0.0 109.1 jit_solution(1040929760812003151)
XLA Ops:
  0.6 104.1 %shard_map.75 = (bf16[128,4096]{1,0:T(8,128)(2,1)}, f32[4,4096]{1,0:T(4,128)}, f32[4,1024]{1,0:T(4,128)}, f32[4,1024]{1,0:T(4,128)}) custom-call(bf16[128,4096]{1,0:T(8,128)(2,1)} %q_hbm.1, bf16[128,1024]{1,0:T(8,128)(2,1)} %k_hbm.1, bf16[128,1024]{1,0:T(8,128)(2,1)} %v_hbm.1, bf16[128,4096]{1,0:T(8,128)(2,1)} %do_hbm.1), custom_call_target="tpu_custom_call" | custom-call | tf_op jit(solution)/shard_map/pallas_call | solution.py:502
  104.7 0.0 copy-start
  104.7 2.3 %copy.12 = bf16[128,4096]{1,0:T(8,128)(2,1)} copy(bf16[128,4096]{1,0:T(8,128)(2,1)} %get-tuple-element.8) | data formatting | bytes 2097152
  107.0 0.0 copy-done
  107.1 0.0 copy-start.2
  107.1 0.6 copy.13
  107.7 0.1 copy-done.2
  107.8 0.0 copy-start.1
  107.8 0.6 copy.14
  108.4 0.1 copy-done.1
  108.5 0.6 copy.15
Async XLA Ops:
  104.7 2.3 %copy-start = (f32[4,4096]{1,0:T(4,128)S(1)}, f32[4,4096]{1,0:T(4,128)}, u32[]{:S(2)}) copy-start(f32[4,4096]{1,0:T(4,128)} %get-tuple-element.9) | copy-start | bytes 196612
  107.1 0.7 copy-start.2
  107.8 0.7 copy-start.1
